TPU v7x, 256 devices: a whole 4x4x8 slice. The times are simulated.
256 devices in a mesh: blk: 64 (over y_lo, z, x), rep: 4 (over y_hi, core).
Axes of the slice: x: 4, y: 4 (y_hi: 2, y_lo: 2; y = y_hi * 2 + y_lo), z: 8, core: 2. Of those that a mesh axis runs over, the one named last changes fastest.
Arguments:
- features: bfloat16 [262144, 128], P(('blk', 'rep')), may hold values from -6 to 6
- weight: bfloat16 [128, 512], replicated, may hold values from -0.5 to 0.5
- bias: float32 [512], replicated, may hold values from -3 to 3
- tile_values: bfloat16 [262144, 4096], P(('blk', 'rep')), may hold values from -0.125 to 0.125
- tile_cols: int32 [2048, 32], P(('blk', 'rep')), may hold values from 0 to 95, as said below
- tile_counts: int32 [2048], P(('blk', 'rep')), may hold values from 1 to 32, as said below
- out_grad: bfloat16 [262144, 512], P(('blk', 'rep')), may hold values from -6 to 6
Outputs:
- activations: bfloat16 [262144, 512], P(('blk', 'rep'))
- feature_grad: float32 [262144, 128], P(('blk', 'rep'))
- weight_grad: float32 [128, 512], replicated
- bias_grad: float32 [512], replicated
Inputs may be any that keep to these rules, and one draw needn't show every extreme that they name: `tile_cols`: within one row tile the 32 entries are different. `tile_counts`: slots 0 to count - 1 of a row tile are live.
All inputs are finite; a program needn't handle non-finite values.
Results may differ from a plain program's by a relative error of at most 0.0059.
Values may be sent and summed in bfloat16 or wider, within the bound.
No kernel may reach another device: no remote copies, remote signals or barrier semaphores. Data moves between devices by JAX's collectives and lax.ppermute only.
A program may use at most 128 MiB of HBM per device.

v0:
```python
import math
import jax
import jax.numpy as jnp
from jax import lax
from jax.sharding import PartitionSpec as P

TILE = 128
REACH = 1
SLOTS = 32


def passed_along(value, axis, steps):
    count = lax.axis_size(axis)
    pairs = [(source, (source + steps) % count) for source in range(count)]
    return lax.ppermute(value, axis, pairs)


def in_blocks(shard, dim, length):
    before, after = (shard.shape[:dim], shard.shape[dim + 1 :])
    return jnp.moveaxis(shard.reshape(*before, length, -1, *after), dim, 0)


def summed_on_arrival(shard, axis, dim):
    length = lax.axis_size(axis)
    pieces = lax.all_to_all(in_blocks(shard, dim, length), axis, 0, 0, tiled=True)
    return jnp.sum(pieces, axis=0)


def gelu_parts(pre_act):
    inner = 0.7978845608028654 * (pre_act + 0.044715 * pre_act * pre_act * pre_act)
    tangent = jnp.tanh(inner)
    value_part = 0.5 * pre_act * (1.0 + tangent)
    slope = 0.5 * (1.0 + tangent) + 0.5 * pre_act * (
        1.0 - tangent * tangent
    ) * 0.7978845608028654 * (1.0 + 0.134145 * pre_act * pre_act)
    return (value_part, slope)


def on_device(features, weight, bias, tile_values, tile_cols, tile_counts, out_grad):
    rows_dev, in_dim = features.shape
    row_tiles = rows_dev // TILE
    group_size = lax.axis_size("rep")
    block_rows = rows_dev * group_size
    nodes = block_rows * lax.axis_size("blk")
    offsets = list(range(-REACH, REACH + 1))
    pieces = []
    for offset_now in offsets:
        if offset_now == 0:
            pieces.append(features)
        else:
            pieces.append(passed_along(features, "blk", -offset_now))
    stacked = jnp.stack(pieces)
    window = lax.all_gather(stacked, "rep", axis=1, tiled=True).reshape(-1, in_dim)
    window_tiles = window.reshape(-1, TILE, in_dim)
    is_live = jnp.arange(SLOTS)[None, :] < tile_counts[:, None]
    gathered = window_tiles[tile_cols]
    gathered = jnp.where(is_live[:, :, None, None], gathered, jnp.zeros((), gathered.dtype))
    gathered = gathered.reshape(row_tiles, SLOTS * TILE, in_dim)
    values = tile_values.reshape(row_tiles, TILE, SLOTS * TILE)
    summed = jnp.einsum(
        "rik,rkf->rif", values, gathered, preferred_element_type=jnp.float32
    ).reshape(rows_dev, in_dim)
    aggregated = summed.astype(jnp.bfloat16)
    pre_act = jnp.dot(aggregated, weight, preferred_element_type=jnp.float32) + bias
    value_part, slope = gelu_parts(pre_act)
    activations = value_part.astype(jnp.bfloat16)
    pre_grad = (out_grad.astype(jnp.float32) * slope).astype(jnp.bfloat16)
    factor = 1.0 / math.sqrt(nodes)
    local_weight = (
        lax.dot_general(
            aggregated, pre_grad, (((0,), (0,)), ((), ())), preferred_element_type=jnp.float32
        )
        * factor
    )
    local_bias = jnp.sum(pre_grad.astype(jnp.float32), axis=0) * factor
    weight_grad, bias_grad = lax.psum((local_weight, local_bias), ("blk", "rep"))
    row_grad = lax.dot_general(
        pre_grad, weight, (((1,), (1,)), ((), ())), preferred_element_type=jnp.float32
    ).astype(jnp.bfloat16)
    grad_tiles = row_grad.reshape(row_tiles, TILE, in_dim)
    partial_value = jnp.einsum(
        "rik,rif->rkf", values, grad_tiles, preferred_element_type=jnp.float32
    )
    partial_value = partial_value.reshape(row_tiles, SLOTS, TILE, in_dim)
    partial_value = jnp.where(
        is_live[:, :, None, None], partial_value, jnp.zeros((), partial_value.dtype)
    )
    window_count = len(offsets) * block_rows // TILE
    placed = (
        jnp.zeros((window_count, TILE, in_dim), jnp.float32)
        .at[tile_cols.reshape(-1)]
        .add(partial_value.reshape(-1, TILE, in_dim))
    )
    terms = placed.reshape(len(offsets), block_rows, in_dim)
    block_total = terms[REACH]
    for position, offset_now in enumerate(offsets):
        if offset_now != 0:
            block_total = block_total + passed_along(
                terms[position].astype(jnp.bfloat16), "blk", offset_now
            ).astype(jnp.float32)
    feature_grad = summed_on_arrival(block_total, "rep", 0)
    return (activations, feature_grad, weight_grad, bias_grad)


def solution(mesh):
    in_specs = (
        P(("blk", "rep"), None),
        P(),
        P(),
        P(("blk", "rep"), None),
        P(("blk", "rep"), None),
        P(("blk", "rep")),
        P(("blk", "rep"), None),
    )
    out_specs = (P(("blk", "rep"), None), P(("blk", "rep"), None), P(), P())
    return jax.shard_map(
        on_device, mesh=mesh, in_specs=in_specs, out_specs=out_specs, check_vma=False
    )
```

profile of v0, /device:TPU:2, one launch (start us, length us, event | category | flops | bytes accessed | tf_op | source)
XLA Modules:
  0.0 501.1 jit_solution(1405045156096830641)
XLA Ops:
  7.2 1.6 collective-permute-start
  9.6 5.9 %collective-permute-done = bf16[1024,128]{1,0:T(8,128)(2,1)S(1)} collective-permute-done((bf16[1024,128]{1,0:T(8,128)(2,1)}, bf16[1024,128]{1,0:T(8,128)(2,1)S(1)}, u32[]{:S(2)}, u32[]{:S(2)}) %collective-permute-start) | collective-permute-done | bytes 262176 | tf_op jit(solution)/shard_map/ppermute | solution.py:15
  15.6 1.2 collective-permute-done.1
  16.8 1.9 pad_maximum_fusion
  21.3 37.8 %all-gather.2.cloned.1.call-done = bf16[3,4096,128]{2,1,0:T(8,128)(2,1)} async-done(((bf16[3,1024,128]{2,1,0:T(8,128)(2,1)}), bf16[3,4096,128]{2,1,0:T(8,128)(2,1)}) %all-gather.2.cloned.1.call-update) | async-done | bytes 3145744 | tf_op jit(solution)/shard_map/all_gather | solution.py:53
  59.0 10.5 %gather_fusion = bf16[256,128,128]{2,1,0:T(8,128)(2,1)} fusion(bf16[96,128,128]{2,1,0:T(8,128)(2,1)} %bitcast.41, s32[1024]{0:T(1024)S(1)} %pad_clamp_fusion), kind=kCustom, calls=%fused_computation | custom fusion | bytes 16778240 | tf_op jit(solution)/shard_map/gather | solution.py:56
  69.6 16.3 %bitcast_select_fusion = bf16[8,4096,128]{2,1,0:T(8,128)(2,1)S(1)} fusion(pred[8,4096]{1,0:T(8,128)(4,1)S(1)} %broadcast_bitcast_fusion, bf16[8,4096,128]{2,1,0:T(8,128)(2,1)} %bitcast.40), kind=kLoop, calls=%fused_computation.3 | loop fusion | flops 4194304 | bytes 16809984 | tf_op jit(solution)/shard_map/jit(_where)/select_n | solution.py:57
  85.9 5.8 %convolution_convert_fusion = bf16[8,128,128]{1,2,0:T(8,128)(2,1)S(1)} fusion(bf16[8,128,4096]{2,1,0:T(8,128)(2,1)} %bitcast.36, bf16[8,4096,128]{2,1,0:T(8,128)(2,1)S(1)} %bitcast_select_fusion), kind=kOutput, calls=%fused_computation.18 | convolution fusion | flops 1073872896 | bytes 17039360 | tf_op jit(solution)/shard_map/rik,rkf->rif/dot_general | solution.py:60
  91.8 2.7 convert_reduce_fusion
  95.6 8.1 %convolution_bitcast_fusion = f32[8,4096,128]{1,2,0:T(8,128)} fusion(bf16[8,128,128]{2,1,0:T(8,128)(2,1)S(1)} %bitcast.42, bf16[8,128,4096]{2,1,0:T(8,128)(2,1)S(1)} %bitcast.39), kind=kOutput, calls=%fused_computation.2 | convolution fusion | flops 1073741824 | bytes 25427968 | tf_op jit(solution)/shard_map/rik,rif->rkf/dot_general | solution.py:81
  103.7 17.4 %copy.17 = f32[8,4096,128]{2,1,0:T(8,128)} copy(f32[8,4096,128]{1,2,0:T(8,128)} %convolution_bitcast_fusion) | data formatting | bytes 33554432 | tf_op jit(solution)/shard_map/rik,rif->rkf/dot_general | solution.py:81
  121.0 11.6 %broadcast_select_fusion = f32[256,128,128]{2,1,0:T(8,128)} fusion(f32[256,128,128]{2,1,0:T(8,128)} %bitcast.35, pred[256]{0:T(512)(128)(4,1)S(1)} %lt.47), kind=kLoop, calls=%fused_computation.4 | loop fusion | flops 4194304 | bytes 33554688 | tf_op jit(solution)/shard_map/jit(_where)/select_n | solution.py:85
  132.7 3.4 broadcast_in_dim.45
  136.1 52.3 %scatter_fusion = f32[96,128,128]{2,1,0:T(8,128)} fusion(f32[96,128,128]{2,1,0:T(8,128)} %broadcast_in_dim.45, s32[256]{0:T(256)S(1)} %bitcast.50, f32[256,128,128]{2,1,0:T(8,128)} %broadcast_select_fusion), kind=kCustom, calls=%fused_computation.1 | custom fusion | flops 4194304 | bytes 50332672 | tf_op jit(solution)/shard_map/scatter-add | solution.py:92
  188.4 3.5 convert.4
  192.6 1.6 collective-permute-start.3
  194.2 1.7 slice.19
  195.9 21.5 %collective-permute-done.2 = bf16[4096,128]{1,0:T(8,128)(2,1)S(1)} collective-permute-done((bf16[4096,128]{1,0:T(8,128)(2,1)S(1)}, bf16[4096,128]{1,0:T(8,128)(2,1)S(1)}, u32[]{:S(2)}, u32[]{:S(2)}) %collective-permute-start.2) | collective-permute-done | bytes 1048608 | tf_op jit(solution)/shard_map/ppermute | solution.py:15
  217.4 3.9 collective-permute-done.3
  221.3 1.6 fusion.7
  222.9 3.6 all-to-all-start
  227.6 96.5 %psum.15 = f32[512]{0:T(512)} all-reduce(f32[512]{0:T(512)S(1)} %broadcast_multiply_fusion), channel_id=1, replica_groups=mesh['blk'=64,'rep'=4] {'blk','rep'}, use_global_device_ids=true, to_apply=%region_4.5 | all-reduce | flops 512 | bytes 4096 | tf_op jit(solution)/shard_map/psum | solution.py:76
  325.1 167.6 %all-reduce.2.cloned.1.call-done = f32[128,512]{1,0:T(8,128)} async-done(((f32[128,512]{1,0:T(8,128)}), f32[128,512]{1,0:T(8,128)}) %all-reduce.2.cloned.1.call-update) | async-done | bytes 262160 | tf_op jit(solution)/shard_map/psum | solution.py:76
  492.6 1.7 copy.21
  (34 shorter events, 7.3 us)
Async XLA Ops:
  7.2 84.6 %copy-start = (bf16[128,512]{1,0:T(8,128)(2,1)S(1)}, bf16[128,512]{1,0:T(8,128)(2,1)}, u32[]{:S(2)}) copy-start(bf16[128,512]{1,0:T(8,128)(2,1)} %param.8) | copy-start | bytes 393220
  7.2 51.9 %all-gather.2.cloned.1.call-start = ((), (), s32[]{:S(2)}) async-start(), calls=%async_computation.1 | async-start | bytes 3932160 | tf_op jit(solution)/shard_map/all_gather | solution.py:53
  7.2 8.3 %collective-permute-start = (bf16[1024,128]{1,0:T(8,128)(2,1)}, bf16[1024,128]{1,0:T(8,128)(2,1)S(1)}, u32[]{:S(2)}, u32[]{:S(2)}) collective-permute-start(bf16[1024,128]{1,0:T(8,128)(2,1)} %param.7), channel_id=1, source_target_pairs={{0,4},{4,8},{8,12},{12,16},{16,20},{20,24},{24,28},{28,32},{32,36}... | collective-permute-start | bytes 786440 | tf_op jit(solution)/shard_map/ppermute | solution.py:15
  8.8 8.0 %collective-permute-start.1 = (bf16[1024,128]{1,0:T(8,128)(2,1)}, bf16[1024,128]{1,0:T(8,128)(2,1)S(1)}, u32[]{:S(2)}, u32[]{:S(2)}) collective-permute-start(bf16[1024,128]{1,0:T(8,128)(2,1)} %param.7), channel_id=1, source_target_pairs={{0,252},{4,0},{8,4},{12,8},{16,12},{20,16},{24,20},{28,24},{32,28}... | collective-permute-start | bytes 786440 | tf_op jit(solution)/shard_map/ppermute | solution.py:15
  85.9 5.9 %copy-start.2 = (bf16[1024,512]{1,0:T(8,128)(2,1)S(1)}, bf16[1024,512]{1,0:T(8,128)(2,1)}, u32[]{:S(2)}) copy-start(bf16[1024,512]{1,0:T(8,128)(2,1)} %param.13) | copy-start | bytes 3145732
  85.9 5.9 %copy-start.3 = (f32[512]{0:T(512)S(1)}, f32[512]{0:T(512)}, u32[]{:S(2)}) copy-start(f32[512]{0:T(512)} %param.9) | copy-start | bytes 6148
  91.7 3.2 slice-start
  91.7 3.8 slice-start.1
  192.1 25.3 %collective-permute-start.2 = (bf16[4096,128]{1,0:T(8,128)(2,1)S(1)}, bf16[4096,128]{1,0:T(8,128)(2,1)S(1)}, u32[]{:S(2)}, u32[]{:S(2)}) collective-permute-start(bf16[4096,128]{1,0:T(8,128)(2,1)S(1)} %bitcast.46), channel_id=1, source_target_pairs={{0,252},{4,0},{8,4},{12,8},{16,12},{20,16},{24,20},{28,24},{32,28}... | collective-permute-start | bytes 3145736 | tf_op jit(solution)/shard_map/ppermute | solution.py:15
  192.6 28.7 %collective-permute-start.3 = (bf16[4096,128]{1,0:T(8,128)(2,1)S(1)}, bf16[4096,128]{1,0:T(8,128)(2,1)S(1)}, u32[]{:S(2)}, u32[]{:S(2)}) collective-permute-start(bf16[4096,128]{1,0:T(8,128)(2,1)S(1)} %bitcast.45), channel_id=1, source_target_pairs={{0,4},{4,8},{8,12},{12,16},{16,20},{20,24},{24,28},{28,32},{32,36}... | collective-permute-start | bytes 3145736 | tf_op jit(solution)/shard_map/ppermute | solution.py:15
  222.9 101.3 %all-to-all-start = ((f32[4,1024,128]{2,1,0:T(8,128)}), f32[4,1024,128]{2,1,0:T(8,128)S(1)}, u32[]{:S(2)}, u32[]{:S(2)}) async-start(f32[4,1024,128]{2,1,0:T(8,128)} %bitcast.16), calls=%async_computation | async-start | bytes 4194304 | tf_op jit(solution)/shard_map/all_to_all | solution.py:25
  226.5 267.8 %copy-start.1 = (bf16[128,512]{1,0:T(8,128)(2,1)S(1)}, bf16[128,512]{1,0:T(8,128)(2,1)}, u32[]{:S(2)}) copy-start(bf16[128,512]{1,0:T(8,128)(2,1)} %param.8) | copy-start | bytes 393220
  226.5 266.1 %all-reduce.2.cloned.1.call-start = ((), (), s32[]{:S(2)}) async-start(), calls=%async_computation.2 | async-start | bytes 524288 | tf_op jit(solution)/shard_map/psum | solution.py:76
Sparse Core Ops, SparseCore 0:
  18.8 40.1 all-gather.1
  233.3 259.2 all-reduce.1
where the time goes:
time: 502 us; the launch traced here: 501 us
  waiting for transfers between devices  238 us (47%)
  blocking collectives  96.5 us (19%)
  other arithmetic  89.6 us (18%)
  local copies, waits for them, and re-layouts  36.7 us (7%)
  matrix products  18.1 us (4%)
  between operations  14.2 us (3%)
  starting transfers between devices  8.2 us (2%)
    psum x1, waiting for transfers between devices, on_device(): lax.psum((local_weight, local_bias), ('blk', 'rep'))  168 us
    psum x1, blocking collectives, on_device(): lax.psum((local_weight, local_bias), ('blk', 'rep'))  96.5 us
    scatter-add x1, other arithmetic, on_device(): placed = jnp.zeros((window_count, TILE, in_dim), jnp.float32).at[tile_col...  52.3 us
    all_gather x1, waiting for transfers between devices, on_device(): lax.all_gather(stacked, 'rep', axis=1, tiled=True).reshape(-1, in_dim)  37.8 us
    ppermute x4, waiting for transfers between devices, passed_along(): return lax.ppermute(value, axis, pairs)  32.5 us
    dot_general x1, local copies, waits for them, and re-layouts, on_device(): jnp.einsum('rik,rif->rkf', values, grad_tiles, preferred_element_type=jnp...  17.4 us
    select_n x1, other arithmetic, on_device(): jnp.where(is_live[:, :, None, None], gathered, jnp.zeros((), gathered.dty...  16.3 us
    select_n x1, other arithmetic, on_device(): jnp.where(is_live[:, :, None, None], partial_value, jnp.zeros((), partial...  11.6 us
  transfers between devices with their start and end apart: 7, of which 6 were waited for; matrix products, arithmetic and copies ran while one was open for 1% of the time, Pallas kernels for 0%

commit v1 on v0

--- a/solution.py
+++ b/solution.py
@@ -73,7 +73,7 @@
         * factor
     )
     local_bias = jnp.sum(pre_grad.astype(jnp.float32), axis=0) * factor
-    weight_grad, bias_grad = lax.psum((local_weight, local_bias), ("blk", "rep"))
+    weight_grad, bias_grad = lax.psum(lax.psum((local_weight, local_bias), "rep"), "blk")
     row_grad = lax.dot_general(
         pre_grad, weight, (((1,), (1,)), ((), ())), preferred_element_type=jnp.float32
     ).astype(jnp.bfloat16)

time: 502 us -> 848 us (1.69)
  waiting for transfers between devices: 238 us -> 517 us
  blocking collectives: 96.5 us -> 162 us
    psum x1 -> x2, waiting for transfers between devices: 168 us -> 447 us  [the longest x1 397 us: on_device(): lax.psum(lax.psum((local_weight, local_bias), 'rep'), 'blk')]
    psum x1 -> x2, blocking collectives: 96.5 us -> 162 us  [the longest x1 154 us: on_device(): lax.psum(lax.psum((local_weight, local_bias), 'rep'), 'blk')]
  transfers between devices with their start and end apart: 7 -> 8, of which waited for: 6 -> 7; matrix products, arithmetic and copies ran while one was open for 1% -> 1% of each run, Pallas kernels for 0% -> 0%
where the time goes in v1:
time: 848 us; the launch traced here: 846 us
  waiting for transfers between devices  517 us (61%)
  blocking collectives  162 us (19%)
  other arithmetic  89.7 us (11%)
  local copies, waits for them, and re-layouts  36.7 us (4%)
  matrix products  18.1 us (2%)
  between operations  13.9 us (2%)
    psum x1, waiting for transfers between devices, on_device(): lax.psum(lax.psum((local_weight, local_bias), 'rep'), 'blk')  397 us
    psum x1, blocking collectives, on_device(): lax.psum(lax.psum((local_weight, local_bias), 'rep'), 'blk')  154 us
    scatter-add x1, other arithmetic, on_device(): placed = jnp.zeros((window_count, TILE, in_dim), jnp.float32).at[tile_col...  52.5 us
    psum x1, waiting for transfers between devices, on_device(): lax.psum((local_weight, local_bias), 'rep')  50.5 us
    all_gather x1, waiting for transfers between devices, on_device(): lax.all_gather(stacked, 'rep', axis=1, tiled=True).reshape(-1, in_dim)  37.8 us
    ppermute x4, waiting for transfers between devices, passed_along(): return lax.ppermute(value, axis, pairs)  32.6 us
    dot_general x1, local copies, waits for them, and re-layouts, on_device(): jnp.einsum('rik,rif->rkf', values, grad_tiles, preferred_element_type=jnp...  17.4 us
  transfers between devices with their start and end apart: 8, of which 7 were waited for; matrix products, arithmetic and copies ran while one was open for 1% of the time, Pallas kernels for 0%

profile of v1, /device:TPU:2, one launch (start us, length us, event | category | flops | bytes accessed | tf_op | source)
XLA Modules:
  0.0 846.2 jit_solution(17055073306088103983)
XLA Ops:
  9.6 5.9 collective-permute-done
  16.8 1.9 pad_maximum_fusion
  21.3 37.8 %all-gather.2.cloned.1.call-done = bf16[3,4096,128]{2,1,0:T(8,128)(2,1)} async-done(((bf16[3,1024,128]{2,1,0:T(8,128)(2,1)}), bf16[3,4096,128]{2,1,0:T(8,128)(2,1)}) %all-gather.2.cloned.1.call-update) | async-done | bytes 3145744 | tf_op jit(solution)/shard_map/all_gather | solution.py:53
  59.0 10.5 %gather_fusion = bf16[256,128,128]{2,1,0:T(8,128)(2,1)} fusion(bf16[96,128,128]{2,1,0:T(8,128)(2,1)} %bitcast.41, s32[1024]{0:T(1024)S(1)} %pad_clamp_fusion), kind=kCustom, calls=%fused_computation | custom fusion | bytes 16778240 | tf_op jit(solution)/shard_map/gather | solution.py:56
  69.5 16.3 %bitcast_select_fusion = bf16[8,4096,128]{2,1,0:T(8,128)(2,1)S(1)} fusion(pred[8,4096]{1,0:T(8,128)(4,1)S(1)} %broadcast_bitcast_fusion, bf16[8,4096,128]{2,1,0:T(8,128)(2,1)} %bitcast.40), kind=kLoop, calls=%fused_computation.3 | loop fusion | flops 4194304 | bytes 16809984 | tf_op jit(solution)/shard_map/jit(_where)/select_n | solution.py:57
  85.9 5.8 convolution_convert_fusion
  91.7 2.7 convert_reduce_fusion
  95.5 8.1 convolution_bitcast_fusion
  103.6 17.4 %copy.17 = f32[8,4096,128]{2,1,0:T(8,128)} copy(f32[8,4096,128]{1,2,0:T(8,128)} %convolution_bitcast_fusion) | data formatting | bytes 33554432 | tf_op jit(solution)/shard_map/rik,rif->rkf/dot_general | solution.py:81
  121.0 11.6 %broadcast_select_fusion = f32[256,128,128]{2,1,0:T(8,128)} fusion(f32[256,128,128]{2,1,0:T(8,128)} %bitcast.35, pred[256]{0:T(512)(128)(4,1)S(1)} %lt.47), kind=kLoop, calls=%fused_computation.4 | loop fusion | flops 4194304 | bytes 33554688 | tf_op jit(solution)/shard_map/jit(_where)/select_n | solution.py:85
  132.6 3.4 broadcast_in_dim.45
  136.1 52.5 %scatter_fusion = f32[96,128,128]{2,1,0:T(8,128)} fusion(f32[96,128,128]{2,1,0:T(8,128)} %broadcast_in_dim.45, s32[256]{0:T(256)S(1)} %bitcast.50, f32[256,128,128]{2,1,0:T(8,128)} %broadcast_select_fusion), kind=kCustom, calls=%fused_computation.1 | custom fusion | flops 4194304 | bytes 50332672 | tf_op jit(solution)/shard_map/scatter-add | solution.py:92
  188.5 3.5 convert.4
  192.7 1.6 collective-permute-start.3
  194.3 1.7 slice.19
  196.0 21.4 %collective-permute-done.2 = bf16[4096,128]{1,0:T(8,128)(2,1)S(1)} collective-permute-done((bf16[4096,128]{1,0:T(8,128)(2,1)S(1)}, bf16[4096,128]{1,0:T(8,128)(2,1)S(1)}, u32[]{:S(2)}, u32[]{:S(2)}) %collective-permute-start.2) | collective-permute-done | bytes 1048608 | tf_op jit(solution)/shard_map/ppermute | solution.py:15
  217.5 4.0 collective-permute-done.3
  221.5 1.6 fusion.7
  223.1 3.6 all-to-all-start
  227.9 50.5 %all-reduce.3.cloned.1.call-done = f32[128,512]{1,0:T(8,128)} async-done(((f32[128,512]{1,0:T(8,128)}), f32[128,512]{1,0:T(8,128)}) %all-reduce.3.cloned.1.call-update) | async-done | bytes 262160 | tf_op jit(solution)/shard_map/psum | solution.py:76
  278.4 7.7 psum.30
  286.1 154.4 %psum.31 = f32[512]{0:T(512)} all-reduce(f32[512]{0:T(512)S(1)} %psum.30), channel_id=1, replica_groups=mesh['blk'=64,'rep'=4] {'blk'}, use_global_device_ids=true, to_apply=%region_6.7 | all-reduce | flops 512 | bytes 4096 | tf_op jit(solution)/shard_map/psum | solution.py:76
  441.5 396.5 %all-reduce.5.cloned.1.call-done = f32[128,512]{1,0:T(8,128)} async-done(((f32[128,512]{1,0:T(8,128)}), f32[128,512]{1,0:T(8,128)}) %all-reduce.5.cloned.1.call-update) | async-done | bytes 262160 | tf_op jit(solution)/shard_map/psum | solution.py:76
  838.0 1.7 copy.22
  (38 shorter events, 10.1 us)
Async XLA Ops:
  7.2 84.5 %copy-start = (bf16[128,512]{1,0:T(8,128)(2,1)S(1)}, bf16[128,512]{1,0:T(8,128)(2,1)}, u32[]{:S(2)}) copy-start(bf16[128,512]{1,0:T(8,128)(2,1)} %param.8) | copy-start | bytes 393220
  7.2 51.9 %all-gather.2.cloned.1.call-start = ((), (), s32[]{:S(2)}) async-start(), calls=%async_computation.1 | async-start | bytes 3932160 | tf_op jit(solution)/shard_map/all_gather | solution.py:53
  7.2 8.3 collective-permute-start
  8.8 8.0 collective-permute-start.1
  85.8 5.9 copy-start.2
  85.9 5.9 copy-start.3
  91.7 3.2 slice-start
  91.7 3.8 slice-start.1
  192.2 25.3 %collective-permute-start.2 = (bf16[4096,128]{1,0:T(8,128)(2,1)S(1)}, bf16[4096,128]{1,0:T(8,128)(2,1)S(1)}, u32[]{:S(2)}, u32[]{:S(2)}) collective-permute-start(bf16[4096,128]{1,0:T(8,128)(2,1)S(1)} %bitcast.46), channel_id=1, source_target_pairs={{0,252},{4,0},{8,4},{12,8},{16,12},{20,16},{24,20},{28,24},{32,28}... | collective-permute-start | bytes 3145736 | tf_op jit(solution)/shard_map/ppermute | solution.py:15
  192.7 28.7 %collective-permute-start.3 = (bf16[4096,128]{1,0:T(8,128)(2,1)S(1)}, bf16[4096,128]{1,0:T(8,128)(2,1)S(1)}, u32[]{:S(2)}, u32[]{:S(2)}) collective-permute-start(bf16[4096,128]{1,0:T(8,128)(2,1)S(1)} %bitcast.45), channel_id=1, source_target_pairs={{0,4},{4,8},{8,12},{12,16},{16,20},{20,24},{24,28},{28,32},{32,36}... | collective-permute-start | bytes 3145736 | tf_op jit(solution)/shard_map/ppermute | solution.py:15
  223.1 217.4 %all-to-all-start = ((f32[4,1024,128]{2,1,0:T(8,128)}), f32[4,1024,128]{2,1,0:T(8,128)S(1)}, u32[]{:S(2)}, u32[]{:S(2)}) async-start(f32[4,1024,128]{2,1,0:T(8,128)} %bitcast.16), calls=%async_computation | async-start | bytes 4194304 | tf_op jit(solution)/shard_map/all_to_all | solution.py:25
  226.7 613.0 %copy-start.1 = (bf16[128,512]{1,0:T(8,128)(2,1)S(1)}, bf16[128,512]{1,0:T(8,128)(2,1)}, u32[]{:S(2)}) copy-start(bf16[128,512]{1,0:T(8,128)(2,1)} %param.8) | copy-start | bytes 393220
  226.7 51.7 %all-reduce.3.cloned.1.call-start = ((), (), s32[]{:S(2)}) async-start(), calls=%async_computation.2 | async-start | bytes 524288 | tf_op jit(solution)/shard_map/psum | solution.py:76
  227.8 610.2 %all-reduce.5.cloned.1.call-start = ((), (), s32[]{:S(2)}) async-start(), calls=%async_computation.3 | async-start | bytes 524288 | tf_op jit(solution)/shard_map/psum | solution.py:76
Sparse Core Ops, SparseCore 0:
  18.8 40.1 all-gather.1
  230.7 47.6 all-reduce.2
  281.0 556.9 all-reduce.4
